TPU v7x, 32 devices: a whole 2x2x4 slice. The times are simulated.
32 devices in a mesh: groups: 2 (over y), obs: 4 (over z), hid: 2 (over x), rep: 2 (over core).
Axes of the slice: x: 2, y: 2, z: 4, core: 2. Of those that a mesh axis runs over, the one named last changes fastest.
Arguments:
- particles: float32 [8, 128, 512], P(('groups', 'obs')), parts along dimension 0, may hold values from -6 to 6
- obs_embed: bfloat16 [32768, 256], P(('groups', 'obs', 'rep')), parts along dimension 0, may hold values from -6 to 6
- step_index: int32 [2], P('groups'), parts along dimension 0, may hold values from 1 to 63
- noise: float32 [8, 128, 512], P('groups', 'obs'), parts along dimension 0, may hold values from -6 to 6
- w_query: bfloat16 [512, 2048], P(None, 'hid'), may hold values from -0.25 to 0.25
- w_key: bfloat16 [256, 2048], P(None, 'hid'), may hold values from -0.375 to 0.375
- w_value: bfloat16 [256, 2048], P(None, 'hid'), may hold values from -0.375 to 0.375
- w_time: bfloat16 [256, 16], P(None, 'hid'), may hold values from -0.375 to 0.375
- w_score: bfloat16 [2048, 512], P('hid'), may hold values from -0.0009765625 to 0.0009765625
- prior_in: bfloat16 [512, 2048], P(None, 'hid'), may hold values from -0.25 to 0.25
- prior_time: bfloat16 [256, 2048], P(None, 'hid'), may hold values from -0.375 to 0.375
- prior_out: bfloat16 [2048, 512], P('hid'), may hold values from -7.6293945e-06 to 7.6293945e-06
Outputs:
- updated: float32 [8, 128, 512], P('groups', 'obs'), parts along dimension 0
- score_total: float32 [8, 128, 512], P('groups', 'obs'), parts along dimension 0
There are 2 independent parts, one for each index of `groups`. A program takes and returns all parts, laid end to end along the dimension named above; an argument that names none is the same for every part. Nothing has to cross between parts.
All inputs are finite; a program needn't handle non-finite values.
Results may differ from a plain program's by a relative error of at most 0.0042.
Values may be sent and summed in bfloat16 or wider, within the bound.
No kernel may reach another device: no remote copies, remote signals or barrier semaphores. Data moves between devices by JAX's collectives and lax.ppermute only.
A program may use at most 64 MiB of HBM per device.

v0:
```python
import math
import jax
import jax.numpy as jnp
from jax import lax
from jax.sharding import PartitionSpec as P

DH = 128
STEPS = 64
SIG_LO = 0.05
SIG_HI = 1.0


def passed_along(shard, axis, by):
    size = lax.axis_size(axis)
    return lax.ppermute(shard, axis, [(i, (i + by) % size) for i in range(size)])


def plan(step_index, feature_count):
    level = step_index[0].astype(jnp.float32)
    growth = math.log(SIG_HI / SIG_LO) / (STEPS - 1)
    sigma_now = SIG_LO * jnp.exp(growth * level)
    sigma_prev = SIG_LO * jnp.exp(growth * (level - 1.0))
    delta = sigma_now * sigma_now - sigma_prev * sigma_prev
    halves = feature_count // 2
    frequency = jnp.exp(-math.log(1000.0) / halves * jnp.arange(halves).astype(jnp.float32))
    angles = 10.0 * jnp.log(sigma_now) * frequency
    features = jnp.concatenate([jnp.sin(angles), jnp.cos(angles)])[None, :].astype(jnp.bfloat16)
    return (features, delta)


def pair_pool(queries, keys, values, head_bias):
    count = queries.shape[0]
    query_heads = queries.reshape(count, -1, DH)
    key_heads = keys.reshape(keys.shape[0], -1, DH)
    value_heads = values.reshape(values.shape[0], -1, DH)
    scores = jnp.einsum("phd,jhd->phj", query_heads, key_heads, preferred_element_type=jnp.float32)
    weights = jax.nn.silu(scores * (1.0 / math.sqrt(DH)) + head_bias[None, :, None]).astype(
        jnp.bfloat16
    )
    pooled = jnp.einsum("phj,jhd->phd", weights, value_heads, preferred_element_type=jnp.float32)
    return pooled.reshape(count, -1)


def on_device(
    particles,
    obs_embed,
    step_index,
    noise,
    w_query,
    w_key,
    w_value,
    w_time,
    w_score,
    prior_in,
    prior_time,
    prior_out,
):
    obs_count = lax.axis_size("obs")
    rep_count = lax.axis_size("rep")
    features, delta = plan(step_index, w_time.shape[0])
    head_bias = jnp.dot(features, w_time, preferred_element_type=jnp.float32)[0]
    keys = jnp.dot(obs_embed, w_key, preferred_element_type=jnp.float32).astype(jnp.bfloat16)
    values = jnp.dot(obs_embed, w_value, preferred_element_type=jnp.float32).astype(jnp.bfloat16)
    home = particles[0]
    block_rows = home.shape[0]
    width = home.shape[1]
    stripe = block_rows // obs_count
    owned = home.reshape(obs_count, stripe, width)
    theta_owner = lax.all_to_all(owned, "obs", split_axis=0, concat_axis=0, tiled=True)
    moving = home.astype(jnp.bfloat16)

    def pool(travel):
        queries = jnp.dot(travel, w_query, preferred_element_type=jnp.float32).astype(jnp.bfloat16)
        return pair_pool(queries, keys, values, head_bias)

    score_weight = w_score.astype(jnp.float32)

    def turn(turn_index, cycle_state):
        arrived = passed_along(cycle_state[0], "obs", 1)
        totals = passed_along(cycle_state[1], "obs", 1)
        return (arrived, totals + pool(arrived))

    cycle_state = lax.fori_loop(0, obs_count - 1, turn, (moving, pool(moving)))
    pieces = cycle_state[1].reshape(obs_count, stripe, -1)
    flat = pieces.reshape(-1, pieces.shape[-1])
    result = jnp.dot(
        flat, score_weight, precision=lax.Precision.HIGHEST, preferred_element_type=jnp.float32
    )
    pieces = result.reshape(pieces.shape[:-1] + (width,))
    received = lax.all_to_all(pieces, "obs", split_axis=0, concat_axis=0, tiled=True)
    summed = jnp.roll(received, 1, axis=0)
    owner_rows = theta_owner.reshape(block_rows, width)
    share = block_rows // rep_count
    start = lax.axis_index("rep") * share
    my_rows = lax.dynamic_slice_in_dim(owner_rows, start, share, 0).astype(jnp.bfloat16)
    prior_pre = jnp.dot(my_rows, prior_in, preferred_element_type=jnp.float32) + jnp.dot(
        features, prior_time, preferred_element_type=jnp.float32
    )
    prior_hidden = jax.nn.silu(prior_pre).astype(jnp.bfloat16)
    prior_part = jnp.dot(prior_hidden, prior_out, preferred_element_type=jnp.float32)
    total_count = obs_embed.shape[0] * obs_count * rep_count
    scores_flat = summed.reshape(block_rows, width)
    current = lax.dynamic_slice_in_dim(scores_flat, start, share, 0)
    scores_flat = lax.dynamic_update_slice_in_dim(
        scores_flat, current - (total_count - 1) * prior_part, start, 0
    )
    score_total = lax.psum(scores_flat, ("hid", "rep")).reshape(obs_count, stripe, width)
    updated = theta_owner + delta * score_total + jnp.sqrt(delta) * noise
    return (updated, score_total)


def solution(mesh):
    in_specs = (
        P(("groups", "obs"), None, None),
        P(("groups", "obs", "rep"), None),
        P("groups"),
        P("groups", "obs", None),
        P(None, "hid"),
        P(None, "hid"),
        P(None, "hid"),
        P(None, "hid"),
        P("hid", None),
        P(None, "hid"),
        P(None, "hid"),
        P("hid", None),
    )
    out_specs = (P("groups", "obs", None), P("groups", "obs", None))
    return jax.shard_map(
        on_device, mesh=mesh, in_specs=in_specs, out_specs=out_specs, check_vma=False
    )
```

profile of v0, /device:TPU:0, one launch (start us, length us, event | category | flops | bytes accessed | tf_op | source)
XLA Modules:
  0.0 154.7 jit_solution(1549332694135412617)
XLA Ops:
  8.1 0.3 copy-done
  8.4 4.3 %convolution_convert_fusion.2 = bf16[2048,1024]{0,1:T(8,128)(2,1)} fusion(bf16[2048,256]{1,0:T(8,128)(2,1)S(1)} %copy-done, bf16[256,1024]{1,0:T(8,128)(2,1)} %param.20), kind=kOutput, calls=%fused_computation.23 | convolution fusion | flops 1075838976 | bytes 5767168 | tf_op jit(solution)/shard_map/dot_general | solution.py:63
  12.8 3.3 %convolution_convert_fusion.1 = bf16[2048,1024]{0,1:T(8,128)(2,1)} fusion(bf16[2048,256]{1,0:T(8,128)(2,1)S(1)} %copy-done, bf16[256,1024]{1,0:T(8,128)(2,1)S(1)} %copy-done.4), kind=kOutput, calls=%fused_computation.22 | convolution fusion | flops 1075838976 | bytes 5767168 | tf_op jit(solution)/shard_map/dot_general | solution.py:62
  16.1 6.5 %copy.19 = bf16[2048,1024]{1,0:T(8,128)(2,1)} copy(bf16[2048,1024]{0,1:T(8,128)(2,1)} %convolution_convert_fusion.1) | data formatting | bytes 8388608 | tf_op jit(solution)/shard_map/while | solution.py:83
  22.7 0.3 fusion.21
  23.0 8.8 %fusion.20 = f32[8,128,128]{2,1,0:T(8,128)} fusion(bf16[2048,8,128]{0,2,1:T(8,128)(2,1)} %bitcast.116, bf16[2048,8,128]{0,2,1:T(8,128)(2,1)} %bitcast.115, f32[8]{0:T(128)S(1)} %bitcast.124, bf16[16,8,8,128]{3,2,1,0:T(8,128)(2,1)S(1)} %fusion.21), kind=kOutput, calls=%fused_computation.24 | convolution fusion | flops 1088421888 | bytes 9175072 | tf_op jit(solution)/shard_map/phj,jhd->phd/dot_general | solution.py:40
  31.9 56.9 %while.12 = (s32[]{:T(128)}, bf16[128,512]{1,0:T(8,128)(2,1)S(1)}, f32[128,1024]{0,1:T(8,128)}, bf16[512,1024]{1,0:T(8,128)(2,1)S(1)}, bf16[2048,1024]{1,0:T(8,1...) while((s32[]{:T(128)}, bf16[128,512]{1,0:T(8,128)(2,1)S(1)}, ...), condition=%wide.region_1.2_spmd, body=%wide.region_0.1_spmd.sunk | while | flops 1222901760 | bytes 15073477 | solution.py:83
  31.9 3.0 %collective-permute-start = (bf16[128,512]{1,0:T(8,128)(2,1)S(1)}, bf16[128,512]{1,0:T(8,128)(2,1)S(1)}, u32[]{:S(2)}, u32[]{:S(2)}) collective-permute-start(bf16[128,512]{1,0:T(8,128)(2,1)S(1)} %get-tuple-element.115), channel_id=1, source_target_pairs={{0,4},{4,8},{8,12},{12,0},{1,5},{5,9},{9,13},{13,1},{2,6},{6,10},{... | collective-permute-start | bytes 393224 | tf_op jit(solution)/shard_map/while/body/eval_jaxpr/ppermute | solution.py:15
  34.9 1.6 %collective-permute-start.1 = (f32[128,1024]{0,1:T(8,128)}, f32[128,1024]{0,1:T(8,128)S(1)}, u32[]{:S(2)}, u32[]{:S(2)}) collective-permute-start(f32[128,1024]{0,1:T(8,128)} %get-tuple-element.116), channel_id=1, source_target_pairs={{0,4},{4,8},{8,12},{12,0},{1,5},{5,9},{9,13},{13,1},{2,6},{6,10},{... | collective-permute-start | bytes 1572872 | tf_op jit(solution)/shard_map/while/body/eval_jaxpr/ppermute | solution.py:15
  36.5 4.8 %collective-permute-done = bf16[128,512]{1,0:T(8,128)(2,1)S(1)} collective-permute-done((bf16[128,512]{1,0:T(8,128)(2,1)S(1)}, bf16[128,512]{1,0:T(8,128)(2,1)S(1)}, u32[]{:S(2)}, u32[]{:S(2)}) %collective-permute-start) | collective-permute-done | bytes 131104 | tf_op jit(solution)/shard_map/while/body/eval_jaxpr/ppermute | solution.py:15
  41.6 6.3 %fusion.73 = f32[8,128,128]{1,2,0:T(8,128)S(1)} fusion(bf16[2048,8,128]{0,2,1:T(8,128)(2,1)} %bitcast.117, f32[8]{0:T(128)S(1)} %bitcast.125, bf16[16,8,8,128]{3,2,1,0:T(8,128)(2,1)S(1)} %fusion.72, bf16[2048,1024]{1,0:T(8,128)(2,1)} %get-tuple-element.126), kind=kOutput, calls=%fused_computation.8.clone.1 | convolution fusion | flops 1088421888 | bytes 9175072 | tf_op jit(solution)/shard_map/while/body/eval_jaxpr/phj,jhd->phd/dot_general | solution.py:40
  47.9 3.8 %collective-permute-done.1 = f32[128,1024]{0,1:T(8,128)S(1)} collective-permute-done((f32[128,1024]{0,1:T(8,128)}, f32[128,1024]{0,1:T(8,128)S(1)}, u32[]{:S(2)}, u32[]{:S(2)}) %collective-permute-start.1) | collective-permute-done | bytes 524320 | tf_op jit(solution)/shard_map/while/body/eval_jaxpr/ppermute | solution.py:15
  51.6 0.9 bitcast_add_fusion.2
  52.5 1.3 collective-permute-start.1
  53.8 6.9 %collective-permute-done = bf16[128,512]{1,0:T(8,128)(2,1)S(1)} collective-permute-done((bf16[128,512]{1,0:T(8,128)(2,1)S(1)}, bf16[128,512]{1,0:T(8,128)(2,1)S(1)}, u32[]{:S(2)}, u32[]{:S(2)}) %collective-permute-start) | collective-permute-done | bytes 131104 | tf_op jit(solution)/shard_map/while/body/eval_jaxpr/ppermute | solution.py:15
  61.1 6.3 %fusion.73 = f32[8,128,128]{1,2,0:T(8,128)S(1)} fusion(bf16[2048,8,128]{0,2,1:T(8,128)(2,1)} %bitcast.117, f32[8]{0:T(128)S(1)} %bitcast.125, bf16[16,8,8,128]{3,2,1,0:T(8,128)(2,1)S(1)} %fusion.72, bf16[2048,1024]{1,0:T(8,128)(2,1)} %get-tuple-element.126), kind=kOutput, calls=%fused_computation.8.clone.1 | convolution fusion | flops 1088421888 | bytes 9175072 | tf_op jit(solution)/shard_map/while/body/eval_jaxpr/phj,jhd->phd/dot_general | solution.py:40
  67.4 2.9 %collective-permute-done.1 = f32[128,1024]{0,1:T(8,128)S(1)} collective-permute-done((f32[128,1024]{0,1:T(8,128)}, f32[128,1024]{0,1:T(8,128)S(1)}, u32[]{:S(2)}, u32[]{:S(2)}) %collective-permute-start.1) | collective-permute-done | bytes 524320 | tf_op jit(solution)/shard_map/while/body/eval_jaxpr/ppermute | solution.py:15
  70.2 0.9 bitcast_add_fusion.2
  71.1 8.2 %collective-permute-done = bf16[128,512]{1,0:T(8,128)(2,1)S(1)} collective-permute-done((bf16[128,512]{1,0:T(8,128)(2,1)S(1)}, bf16[128,512]{1,0:T(8,128)(2,1)S(1)}, u32[]{:S(2)}, u32[]{:S(2)}) %collective-permute-start) | collective-permute-done | bytes 131104 | tf_op jit(solution)/shard_map/while/body/eval_jaxpr/ppermute | solution.py:15
  79.7 6.3 %fusion.73 = f32[8,128,128]{1,2,0:T(8,128)S(1)} fusion(bf16[2048,8,128]{0,2,1:T(8,128)(2,1)} %bitcast.117, f32[8]{0:T(128)S(1)} %bitcast.125, bf16[16,8,8,128]{3,2,1,0:T(8,128)(2,1)S(1)} %fusion.72, bf16[2048,1024]{1,0:T(8,128)(2,1)} %get-tuple-element.126), kind=kOutput, calls=%fused_computation.8.clone.1 | convolution fusion | flops 1088421888 | bytes 9175072 | tf_op jit(solution)/shard_map/while/body/eval_jaxpr/phj,jhd->phd/dot_general | solution.py:40
  86.0 2.0 %collective-permute-done.1 = f32[128,1024]{0,1:T(8,128)S(1)} collective-permute-done((f32[128,1024]{0,1:T(8,128)}, f32[128,1024]{0,1:T(8,128)S(1)}, u32[]{:S(2)}, u32[]{:S(2)}) %collective-permute-start.1) | collective-permute-done | bytes 524320 | tf_op jit(solution)/shard_map/while/body/eval_jaxpr/ppermute | solution.py:15
  87.9 0.9 bitcast_add_fusion.2
  88.8 2.2 %fusion.36 = f32[128,512]{1,0:T(8,128)S(1)} fusion(f32[128,1024]{0,1:T(8,128)} %get-tuple-element.39, bf16[1024,512]{1,0:T(8,128)(2,1)} %param.22), kind=kOutput, calls=%fused_computation.49 | convolution fusion | flops 805306368 | bytes 1835008 | tf_op jit(solution)/shard_map/dot_general | solution.py:86
  91.0 9.5 %all_to_all.10 = f32[4,32,512]{2,1,0:T(8,128)S(1)} all-to-all(f32[4,32,512]{2,1,0:T(8,128)S(1)} %bitcast.119), channel_id=1, replica_groups=mesh['groups'=2,'obs'=4,'hid'=2,'rep'=2] {'obs'}, dimensions={0} | all-to-all | bytes 524288 | tf_op jit(solution)/shard_map/all_to_all | solution.py:90
  100.5 3.4 %all-to-all-start = ((f32[4,32,512]{2,1,0:T(8,128)}), f32[4,32,512]{2,1,0:T(8,128)S(1)}, u32[]{:S(2)}, u32[]{:S(2)}) async-start(f32[4,32,512]{2,1,0:T(8,128)} %bitcast.120), calls=%async_computation | async-start | bytes 524288 | tf_op jit(solution)/shard_map/all_to_all | solution.py:69
  103.9 1.2 fusion.37
  105.2 5.4 %all-to-all-done = f32[4,32,512]{2,1,0:T(8,128)S(1)} async-done(((f32[4,32,512]{2,1,0:T(8,128)}), f32[4,32,512]{2,1,0:T(8,128)S(1)}, u32[]{:S(2)}, u32[]{:S(2)}) %all-to-all-start) | async-done | bytes 262176 | tf_op jit(solution)/shard_map/all_to_all | solution.py:69
  110.6 1.7 %fusion.23 = f32[128,512]{1,0:T(8,128)S(1)} fusion(f32[128,512]{1,0:T(8,128)S(1)} %bitcast.121, s32[]{:T(128)S(6)} %select_n.2, bf16[1024,512]{1,0:T(8,128)(2,1)S(1)} %copy-done.6, bf16[512,1024]{1,0:T(8,128)(2,1)} %param.23, f32[1024]{0:T(1024)S(1)} %bitcast.123, f32[128,512]{1,0:T(8,128)S(1)} %bitcast.118), kind=kOutput, calls=%fused_computation.30 | convolution fusion | flops 134676480 | bytes 2429952 | tf_op jit(solution)/shard_map/dot_general | solution.py:100
  112.4 0.7 copy-done.3
  113.2 31.3 %all-reduce.2.cloned.1.call-done = f32[4,32,512]{2,1,0:T(8,128)} async-done(((f32[4,32,512]{2,1,0:T(8,128)}), f32[4,32,512]{2,1,0:T(8,128)}) %all-reduce.2.cloned.1.call-update) | async-done | bytes 262160 | tf_op jit(solution)/shard_map/psum | solution.py:107
  144.5 1.7 %multiply_add_fusion = f32[4,32,512]{2,1,0:T(8,128)} fusion(f32[4,32,512]{2,1,0:T(8,128)S(1)} %copy-done.5, f32[4,32,512]{2,1,0:T(8,128)S(1)} %all-to-all-done, f32[4,32,512]{2,1,0:T(8,128)} %all-reduce.2.cloned.1.call-done, f32[]{:T(128)S(6)} %sqrt.3, f32[]{:T(128)} %bitcast.6), kind=kLoop, calls=%fused_computation.34 | loop fusion | flops 262144 | bytes 1048584 | tf_op jit(solution)/shard_map/add | solution.py:108
  146.2 1.7 %copy.57 = f32[4,32,512]{2,1,0:T(8,128)} copy(f32[4,32,512]{2,1,0:T(8,128)} %all-reduce.2.cloned.1.call-done) | data formatting | bytes 524288
  (33 shorter events, 1.3 us)
Async XLA Ops:
  7.2 1.2 copy-start
  8.4 4.4 %copy-start.4 = (bf16[256,1024]{1,0:T(8,128)(2,1)S(1)}, bf16[256,1024]{1,0:T(8,128)(2,1)}, u32[]{:S(2)}) copy-start(bf16[256,1024]{1,0:T(8,128)(2,1)} %param.19) | copy-start | bytes 1572868
  12.8 3.3 %copy-start.2 = (f32[1,128,512]{2,1,0:T(8,128)S(1)}, f32[1,128,512]{2,1,0:T(8,128)}, u32[]{:S(2)}) copy-start(f32[1,128,512]{2,1,0:T(8,128)} %param.14) | copy-start | bytes 786436
  16.1 6.5 %copy-start.7 = (bf16[256,8]{0,1:T(8,128)(2,1)S(1)}, bf16[256,8]{0,1:T(8,128)(2,1)}, u32[]{:S(2)}) copy-start(bf16[256,8]{0,1:T(8,128)(2,1)} %param.21) | copy-start | bytes 12292
  16.1 6.6 %copy-start.1 = (bf16[512,1024]{1,0:T(8,128)(2,1)S(1)}, bf16[512,1024]{1,0:T(8,128)(2,1)}, u32[]{:S(2)}) copy-start(bf16[512,1024]{1,0:T(8,128)(2,1)} %param.18) | copy-start | bytes 3145732
  31.9 9.4 %collective-permute-start = (bf16[128,512]{1,0:T(8,128)(2,1)S(1)}, bf16[128,512]{1,0:T(8,128)(2,1)S(1)}, u32[]{:S(2)}, u32[]{:S(2)}) collective-permute-start(bf16[128,512]{1,0:T(8,128)(2,1)S(1)} %get-tuple-element.115), channel_id=1, source_target_pairs={{0,4},{4,8},{8,12},{12,0},{1,5},{5,9},{9,13},{13,1},{2,6},{6,10},{... | collective-permute-start | bytes 393224 | tf_op jit(solution)/shard_map/while/body/eval_jaxpr/ppermute | solution.py:15
  34.9 16.7 %collective-permute-start.1 = (f32[128,1024]{0,1:T(8,128)}, f32[128,1024]{0,1:T(8,128)S(1)}, u32[]{:S(2)}, u32[]{:S(2)}) collective-permute-start(f32[128,1024]{0,1:T(8,128)} %get-tuple-element.116), channel_id=1, source_target_pairs={{0,4},{4,8},{8,12},{12,0},{1,5},{5,9},{9,13},{13,1},{2,6},{6,10},{... | collective-permute-start | bytes 1572872 | tf_op jit(solution)/shard_map/while/body/eval_jaxpr/ppermute | solution.py:15
  52.5 8.2 %collective-permute-start = (bf16[128,512]{1,0:T(8,128)(2,1)S(1)}, bf16[128,512]{1,0:T(8,128)(2,1)S(1)}, u32[]{:S(2)}, u32[]{:S(2)}) collective-permute-start(bf16[128,512]{1,0:T(8,128)(2,1)S(1)} %get-tuple-element.115), channel_id=1, source_target_pairs={{0,4},{4,8},{8,12},{12,0},{1,5},{5,9},{9,13},{13,1},{2,6},{6,10},{... | collective-permute-start | bytes 393224 | tf_op jit(solution)/shard_map/while/body/eval_jaxpr/ppermute | solution.py:15
  52.5 17.7 %collective-permute-start.1 = (f32[128,1024]{0,1:T(8,128)}, f32[128,1024]{0,1:T(8,128)S(1)}, u32[]{:S(2)}, u32[]{:S(2)}) collective-permute-start(f32[128,1024]{0,1:T(8,128)} %get-tuple-element.116), channel_id=1, source_target_pairs={{0,4},{4,8},{8,12},{12,0},{1,5},{5,9},{9,13},{13,1},{2,6},{6,10},{... | collective-permute-start | bytes 1572872 | tf_op jit(solution)/shard_map/while/body/eval_jaxpr/ppermute | solution.py:15
  71.1 8.2 %collective-permute-start = (bf16[128,512]{1,0:T(8,128)(2,1)S(1)}, bf16[128,512]{1,0:T(8,128)(2,1)S(1)}, u32[]{:S(2)}, u32[]{:S(2)}) collective-permute-start(bf16[128,512]{1,0:T(8,128)(2,1)S(1)} %get-tuple-element.115), channel_id=1, source_target_pairs={{0,4},{4,8},{8,12},{12,0},{1,5},{5,9},{9,13},{13,1},{2,6},{6,10},{... | collective-permute-start | bytes 393224 | tf_op jit(solution)/shard_map/while/body/eval_jaxpr/ppermute | solution.py:15
  71.1 16.8 %collective-permute-start.1 = (f32[128,1024]{0,1:T(8,128)}, f32[128,1024]{0,1:T(8,128)S(1)}, u32[]{:S(2)}, u32[]{:S(2)}) collective-permute-start(f32[128,1024]{0,1:T(8,128)} %get-tuple-element.116), channel_id=1, source_target_pairs={{0,4},{4,8},{8,12},{12,0},{1,5},{5,9},{9,13},{13,1},{2,6},{6,10},{... | collective-permute-start | bytes 1572872 | tf_op jit(solution)/shard_map/while/body/eval_jaxpr/ppermute | solution.py:15
  88.8 21.9 %copy-start.6 = (bf16[1024,512]{1,0:T(8,128)(2,1)S(1)}, bf16[1024,512]{1,0:T(8,128)(2,1)}, u32[]{:S(2)}) copy-start(bf16[1024,512]{1,0:T(8,128)(2,1)} %param.25) | copy-start | bytes 3145732
  88.8 55.7 %copy-start.5 = (f32[4,32,512]{2,1,0:T(8,128)S(1)}, f32[4,32,512]{2,1,0:T(8,128)}, u32[]{:S(2)}) copy-start(f32[4,32,512]{2,1,0:T(8,128)} %param.17) | copy-start | bytes 786436
  100.5 10.2 %all-to-all-start = ((f32[4,32,512]{2,1,0:T(8,128)}), f32[4,32,512]{2,1,0:T(8,128)S(1)}, u32[]{:S(2)}, u32[]{:S(2)}) async-start(f32[4,32,512]{2,1,0:T(8,128)} %bitcast.120), calls=%async_computation | async-start | bytes 524288 | tf_op jit(solution)/shard_map/all_to_all | solution.py:69
  103.9 40.6 %all-reduce.2.cloned.1.call-start = ((), (), s32[]{:S(2)}) async-start(), calls=%async_computation.2 | async-start | bytes 524288 | tf_op jit(solution)/shard_map/psum | solution.py:107
  112.4 0.7 copy-start.3
Sparse Core Ops, SparseCore 0:
  113.2 31.2 all-reduce.1
where the time goes:
time: 155 us
  waiting for transfers between devices  65.3 us (42%)
  matrix products  41.7 us (27%)
  between operations  15.1 us (10%)
  blocking collectives  9.51 us (6%)
  starting transfers between devices  9.34 us (6%)
  local copies, waits for them, and re-layouts  9.31 us (6%)
  other arithmetic  4.42 us (3%)
    psum x1, waiting for transfers between devices, on_device(): lax.psum(scores_flat, ('hid', 'rep')).reshape(obs_count, stripe, width)  31.3 us
    ppermute x6, waiting for transfers between devices, passed_along(): lax.ppermute(shard, axis, [(i, (i + by) % size) for i in range(size)])  28.5 us
    dot_general x4, matrix products, pair_pool(): jnp.einsum('phj,jhd->phd', weights, value_heads, preferred_element_type=j...  27.6 us
    all_to_all x1, blocking collectives, on_device(): lax.all_to_all(pieces, 'obs', split_axis=0, concat_axis=0, tiled=True)  9.51 us
    while x1, local copies, waits for them, and re-layouts, on_device(): cycle_state = lax.fori_loop(0, obs_count - 1, turn, (moving, pool(moving)))  6.51 us
    ppermute x6, starting transfers between devices, passed_along(): lax.ppermute(shard, axis, [(i, (i + by) % size) for i in range(size)])  5.89 us
    all_to_all x1, waiting for transfers between devices, on_device(): lax.all_to_all(owned, 'obs', split_axis=0, concat_axis=0, tiled=True)  5.4 us
    dot_general x1, matrix products, on_device(): jnp.dot(obs_embed, w_value, preferred_element_type=jnp.float32)  4.35 us
  transfers between devices with their start and end apart: 8, of which 8 were waited for; matrix products, arithmetic and copies ran while one was open for 14% of the time, Pallas kernels for 0%

commit v1 on v0

--- a/solution.py
+++ b/solution.py
@@ -8,6 +8,14 @@
 STEPS = 64
 SIG_LO = 0.05
 SIG_HI = 1.0
+
+
+def clear_shards(block_here):
+    mesh_dim = "hid"
+    axis_key = "rep"
+    for k in (axis_key, mesh_dim):
+        block_here = lax.psum(block_here, k)
+    return block_here
 
 
 def passed_along(shard, axis, by):
@@ -104,7 +112,7 @@
     scores_flat = lax.dynamic_update_slice_in_dim(
         scores_flat, current - (total_count - 1) * prior_part, start, 0
     )
-    score_total = lax.psum(scores_flat, ("hid", "rep")).reshape(obs_count, stripe, width)
+    score_total = clear_shards(scores_flat).reshape(obs_count, stripe, width)
     updated = theta_owner + delta * score_total + jnp.sqrt(delta) * noise
     return (updated, score_total)
 

time: 155 us -> 168 us (1.084)
  waiting for transfers between devices: 65.3 us -> 78.3 us
    psum x1 -> x2, waiting for transfers between devices: 31.3 us -> 44.3 us  [clear_shards(): block_here = lax.psum(block_here, k)]
  transfers between devices with their start and end apart: 8 -> 9, of which waited for: 8 -> 9; matrix products, arithmetic and copies ran while one was open for 14% -> 13% of each run, Pallas kernels for 0% -> 0%
where the time goes in v1:
time: 168 us
  waiting for transfers between devices  78.3 us (47%)
  matrix products  41.7 us (25%)
  between operations  15.1 us (9%)
  blocking collectives  9.51 us (6%)
  starting transfers between devices  9.39 us (6%)
  local copies, waits for them, and re-layouts  9.31 us (6%)
  other arithmetic  4.42 us (3%)
    psum x2, waiting for transfers between devices, clear_shards(): block_here = lax.psum(block_here, k)  44.3 us
    ppermute x6, waiting for transfers between devices, passed_along(): lax.ppermute(shard, axis, [(i, (i + by) % size) for i in range(size)])  28.5 us
    dot_general x4, matrix products, pair_pool(): jnp.einsum('phj,jhd->phd', weights, value_heads, preferred_element_type=j...  27.6 us
    all_to_all x1, blocking collectives, on_device(): lax.all_to_all(pieces, 'obs', split_axis=0, concat_axis=0, tiled=True)  9.51 us
    while x1, local copies, waits for them, and re-layouts, on_device(): cycle_state = lax.fori_loop(0, obs_count - 1, turn, (moving, pool(moving)))  6.51 us
    ppermute x6, starting transfers between devices, passed_along(): lax.ppermute(shard, axis, [(i, (i + by) % size) for i in range(size)])  5.89 us
    all_to_all x1, waiting for transfers between devices, on_device(): lax.all_to_all(owned, 'obs', split_axis=0, concat_axis=0, tiled=True)  5.4 us
    dot_general x1, matrix products, on_device(): jnp.dot(obs_embed, w_value, preferred_element_type=jnp.float32)  4.35 us
  transfers between devices with their start and end apart: 9, of which 9 were waited for; matrix products, arithmetic and copies ran while one was open for 13% of the time, Pallas kernels for 0%

profile of v1, /device:TPU:0, one launch (start us, length us, event | category | flops | bytes accessed | tf_op | source)
XLA Modules:
  0.0 167.8 jit_solution(16154696894718025608)
XLA Ops:
  8.1 0.3 copy-done
  8.4 4.3 %convolution_convert_fusion.2 = bf16[2048,1024]{0,1:T(8,128)(2,1)} fusion(bf16[2048,256]{1,0:T(8,128)(2,1)S(1)} %copy-done, bf16[256,1024]{1,0:T(8,128)(2,1)} %param.20), kind=kOutput, calls=%fused_computation.23 | convolution fusion | flops 1075838976 | bytes 5767168 | tf_op jit(solution)/shard_map/dot_general | solution.py:71
  12.8 3.3 %convolution_convert_fusion.1 = bf16[2048,1024]{0,1:T(8,128)(2,1)} fusion(bf16[2048,256]{1,0:T(8,128)(2,1)S(1)} %copy-done, bf16[256,1024]{1,0:T(8,128)(2,1)S(1)} %copy-done.4), kind=kOutput, calls=%fused_computation.22 | convolution fusion | flops 1075838976 | bytes 5767168 | tf_op jit(solution)/shard_map/dot_general | solution.py:70
  16.1 6.5 %copy.19 = bf16[2048,1024]{1,0:T(8,128)(2,1)} copy(bf16[2048,1024]{0,1:T(8,128)(2,1)} %convolution_convert_fusion.1) | data formatting | bytes 8388608 | tf_op jit(solution)/shard_map/while | solution.py:91
  23.0 8.8 %fusion.20 = f32[8,128,128]{2,1,0:T(8,128)} fusion(bf16[2048,8,128]{0,2,1:T(8,128)(2,1)} %bitcast.116, bf16[2048,8,128]{0,2,1:T(8,128)(2,1)} %bitcast.115, f32[8]{0:T(128)S(1)} %bitcast.124, bf16[16,8,8,128]{3,2,1,0:T(8,128)(2,1)S(1)} %fusion.21), kind=kOutput, calls=%fused_computation.24 | convolution fusion | flops 1088421888 | bytes 9175072 | tf_op jit(solution)/shard_map/phj,jhd->phd/dot_general | solution.py:48
  31.9 56.9 %while.12 = (s32[]{:T(128)}, bf16[128,512]{1,0:T(8,128)(2,1)S(1)}, f32[128,1024]{0,1:T(8,128)}, bf16[512,1024]{1,0:T(8,128)(2,1)S(1)}, bf16[2048,1024]{1,0:T(8,1...) while((s32[]{:T(128)}, bf16[128,512]{1,0:T(8,128)(2,1)S(1)}, ...), condition=%wide.region_1.2_spmd, body=%wide.region_0.1_spmd.sunk | while | flops 1222901760 | bytes 15073477 | solution.py:91
  31.9 3.0 %collective-permute-start = (bf16[128,512]{1,0:T(8,128)(2,1)S(1)}, bf16[128,512]{1,0:T(8,128)(2,1)S(1)}, u32[]{:S(2)}, u32[]{:S(2)}) collective-permute-start(bf16[128,512]{1,0:T(8,128)(2,1)S(1)} %get-tuple-element.115), channel_id=1, source_target_pairs={{0,4},{4,8},{8,12},{12,0},{1,5},{5,9},{9,13},{13,1},{2,6},{6,10},{... | collective-permute-start | bytes 393224 | tf_op jit(solution)/shard_map/while/body/eval_jaxpr/ppermute | solution.py:23
  34.9 1.6 collective-permute-start.1
  36.5 4.8 %collective-permute-done = bf16[128,512]{1,0:T(8,128)(2,1)S(1)} collective-permute-done((bf16[128,512]{1,0:T(8,128)(2,1)S(1)}, bf16[128,512]{1,0:T(8,128)(2,1)S(1)}, u32[]{:S(2)}, u32[]{:S(2)}) %collective-permute-start) | collective-permute-done | bytes 131104 | tf_op jit(solution)/shard_map/while/body/eval_jaxpr/ppermute | solution.py:23
  41.6 6.3 %fusion.73 = f32[8,128,128]{1,2,0:T(8,128)S(1)} fusion(bf16[2048,8,128]{0,2,1:T(8,128)(2,1)} %bitcast.117, f32[8]{0:T(128)S(1)} %bitcast.125, bf16[16,8,8,128]{3,2,1,0:T(8,128)(2,1)S(1)} %fusion.72, bf16[2048,1024]{1,0:T(8,128)(2,1)} %get-tuple-element.126), kind=kOutput, calls=%fused_computation.8.clone.1 | convolution fusion | flops 1088421888 | bytes 9175072 | tf_op jit(solution)/shard_map/while/body/eval_jaxpr/phj,jhd->phd/dot_general | solution.py:48
  47.9 3.8 %collective-permute-done.1 = f32[128,1024]{0,1:T(8,128)S(1)} collective-permute-done((f32[128,1024]{0,1:T(8,128)}, f32[128,1024]{0,1:T(8,128)S(1)}, u32[]{:S(2)}, u32[]{:S(2)}) %collective-permute-start.1) | collective-permute-done | bytes 524320 | tf_op jit(solution)/shard_map/while/body/eval_jaxpr/ppermute | solution.py:23
  51.6 0.9 bitcast_add_fusion.2
  52.5 1.3 collective-permute-start.1
  53.8 6.9 %collective-permute-done = bf16[128,512]{1,0:T(8,128)(2,1)S(1)} collective-permute-done((bf16[128,512]{1,0:T(8,128)(2,1)S(1)}, bf16[128,512]{1,0:T(8,128)(2,1)S(1)}, u32[]{:S(2)}, u32[]{:S(2)}) %collective-permute-start) | collective-permute-done | bytes 131104 | tf_op jit(solution)/shard_map/while/body/eval_jaxpr/ppermute | solution.py:23
  61.1 6.3 %fusion.73 = f32[8,128,128]{1,2,0:T(8,128)S(1)} fusion(bf16[2048,8,128]{0,2,1:T(8,128)(2,1)} %bitcast.117, f32[8]{0:T(128)S(1)} %bitcast.125, bf16[16,8,8,128]{3,2,1,0:T(8,128)(2,1)S(1)} %fusion.72, bf16[2048,1024]{1,0:T(8,128)(2,1)} %get-tuple-element.126), kind=kOutput, calls=%fused_computation.8.clone.1 | convolution fusion | flops 1088421888 | bytes 9175072 | tf_op jit(solution)/shard_map/while/body/eval_jaxpr/phj,jhd->phd/dot_general | solution.py:48
  67.4 2.9 %collective-permute-done.1 = f32[128,1024]{0,1:T(8,128)S(1)} collective-permute-done((f32[128,1024]{0,1:T(8,128)}, f32[128,1024]{0,1:T(8,128)S(1)}, u32[]{:S(2)}, u32[]{:S(2)}) %collective-permute-start.1) | collective-permute-done | bytes 524320 | tf_op jit(solution)/shard_map/while/body/eval_jaxpr/ppermute | solution.py:23
  70.2 0.9 bitcast_add_fusion.2
  71.1 8.2 %collective-permute-done = bf16[128,512]{1,0:T(8,128)(2,1)S(1)} collective-permute-done((bf16[128,512]{1,0:T(8,128)(2,1)S(1)}, bf16[128,512]{1,0:T(8,128)(2,1)S(1)}, u32[]{:S(2)}, u32[]{:S(2)}) %collective-permute-start) | collective-permute-done | bytes 131104 | tf_op jit(solution)/shard_map/while/body/eval_jaxpr/ppermute | solution.py:23
  79.7 6.3 %fusion.73 = f32[8,128,128]{1,2,0:T(8,128)S(1)} fusion(bf16[2048,8,128]{0,2,1:T(8,128)(2,1)} %bitcast.117, f32[8]{0:T(128)S(1)} %bitcast.125, bf16[16,8,8,128]{3,2,1,0:T(8,128)(2,1)S(1)} %fusion.72, bf16[2048,1024]{1,0:T(8,128)(2,1)} %get-tuple-element.126), kind=kOutput, calls=%fused_computation.8.clone.1 | convolution fusion | flops 1088421888 | bytes 9175072 | tf_op jit(solution)/shard_map/while/body/eval_jaxpr/phj,jhd->phd/dot_general | solution.py:48
  86.0 2.0 %collective-permute-done.1 = f32[128,1024]{0,1:T(8,128)S(1)} collective-permute-done((f32[128,1024]{0,1:T(8,128)}, f32[128,1024]{0,1:T(8,128)S(1)}, u32[]{:S(2)}, u32[]{:S(2)}) %collective-permute-start.1) | collective-permute-done | bytes 524320 | tf_op jit(solution)/shard_map/while/body/eval_jaxpr/ppermute | solution.py:23
  87.9 0.9 bitcast_add_fusion.2
  88.8 2.2 %fusion.36 = f32[128,512]{1,0:T(8,128)S(1)} fusion(f32[128,1024]{0,1:T(8,128)} %get-tuple-element.39, bf16[1024,512]{1,0:T(8,128)(2,1)} %param.22), kind=kOutput, calls=%fused_computation.49 | convolution fusion | flops 805306368 | bytes 1835008 | tf_op jit(solution)/shard_map/dot_general | solution.py:94
  91.0 9.5 %all_to_all.10 = f32[4,32,512]{2,1,0:T(8,128)S(1)} all-to-all(f32[4,32,512]{2,1,0:T(8,128)S(1)} %bitcast.119), channel_id=1, replica_groups=mesh['groups'=2,'obs'=4,'hid'=2,'rep'=2] {'obs'}, dimensions={0} | all-to-all | bytes 524288 | tf_op jit(solution)/shard_map/all_to_all | solution.py:98
  100.5 3.4 %all-to-all-start = ((f32[4,32,512]{2,1,0:T(8,128)}), f32[4,32,512]{2,1,0:T(8,128)S(1)}, u32[]{:S(2)}, u32[]{:S(2)}) async-start(f32[4,32,512]{2,1,0:T(8,128)} %bitcast.120), calls=%async_computation | async-start | bytes 524288 | tf_op jit(solution)/shard_map/all_to_all | solution.py:77
  103.9 1.2 fusion.37
  105.2 5.4 %all-to-all-done = f32[4,32,512]{2,1,0:T(8,128)S(1)} async-done(((f32[4,32,512]{2,1,0:T(8,128)}), f32[4,32,512]{2,1,0:T(8,128)S(1)}, u32[]{:S(2)}, u32[]{:S(2)}) %all-to-all-start) | async-done | bytes 262176 | tf_op jit(solution)/shard_map/all_to_all | solution.py:77
  110.6 1.7 %fusion.23 = f32[128,512]{1,0:T(8,128)S(1)} fusion(f32[128,512]{1,0:T(8,128)S(1)} %bitcast.121, s32[]{:T(128)S(6)} %select_n.2, bf16[1024,512]{1,0:T(8,128)(2,1)S(1)} %copy-done.6, bf16[512,1024]{1,0:T(8,128)(2,1)} %param.23, f32[1024]{0:T(1024)S(1)} %bitcast.123, f32[128,512]{1,0:T(8,128)S(1)} %bitcast.118), kind=kOutput, calls=%fused_computation.30 | convolution fusion | flops 134676480 | bytes 2429952 | tf_op jit(solution)/shard_map/dot_general | solution.py:108
  112.4 0.7 copy-done.3
  113.1 17.7 %all-reduce.3.cloned.1.call-done = f32[128,512]{1,0:T(8,128)} async-done(((f32[128,512]{1,0:T(8,128)}), f32[128,512]{1,0:T(8,128)}) %all-reduce.3.cloned.1.call-update) | async-done | bytes 262160 | tf_op jit(solution)/shard_map/psum | solution.py:17
  130.9 26.6 %all-reduce.5.cloned.1.call-done = f32[4,32,512]{2,1,0:T(8,128)} async-done(((f32[4,32,512]{2,1,0:T(8,128)}), f32[4,32,512]{2,1,0:T(8,128)}) %all-reduce.5.cloned.1.call-update) | async-done | bytes 262160 | tf_op jit(solution)/shard_map/psum | solution.py:17
  157.6 1.7 %multiply_add_fusion = f32[4,32,512]{2,1,0:T(8,128)} fusion(f32[4,32,512]{2,1,0:T(8,128)S(1)} %copy-done.5, f32[4,32,512]{2,1,0:T(8,128)S(1)} %all-to-all-done, f32[4,32,512]{2,1,0:T(8,128)} %all-reduce.5.cloned.1.call-done, f32[]{:T(128)S(6)} %sqrt.3, f32[]{:T(128)} %bitcast.6), kind=kLoop, calls=%fused_computation.34 | loop fusion | flops 262144 | bytes 1048584 | tf_op jit(solution)/shard_map/add | solution.py:116
  159.3 1.7 copy.58
  (36 shorter events, 1.7 us)
Async XLA Ops:
  7.2 1.2 copy-start
  8.4 4.4 %copy-start.4 = (bf16[256,1024]{1,0:T(8,128)(2,1)S(1)}, bf16[256,1024]{1,0:T(8,128)(2,1)}, u32[]{:S(2)}) copy-start(bf16[256,1024]{1,0:T(8,128)(2,1)} %param.19) | copy-start | bytes 1572868
  12.8 3.3 %copy-start.2 = (f32[1,128,512]{2,1,0:T(8,128)S(1)}, f32[1,128,512]{2,1,0:T(8,128)}, u32[]{:S(2)}) copy-start(f32[1,128,512]{2,1,0:T(8,128)} %param.14) | copy-start | bytes 786436
  16.1 6.5 %copy-start.7 = (bf16[256,8]{0,1:T(8,128)(2,1)S(1)}, bf16[256,8]{0,1:T(8,128)(2,1)}, u32[]{:S(2)}) copy-start(bf16[256,8]{0,1:T(8,128)(2,1)} %param.21) | copy-start | bytes 12292
  16.1 6.6 %copy-start.1 = (bf16[512,1024]{1,0:T(8,128)(2,1)S(1)}, bf16[512,1024]{1,0:T(8,128)(2,1)}, u32[]{:S(2)}) copy-start(bf16[512,1024]{1,0:T(8,128)(2,1)} %param.18) | copy-start | bytes 3145732
  31.9 9.4 %collective-permute-start = (bf16[128,512]{1,0:T(8,128)(2,1)S(1)}, bf16[128,512]{1,0:T(8,128)(2,1)S(1)}, u32[]{:S(2)}, u32[]{:S(2)}) collective-permute-start(bf16[128,512]{1,0:T(8,128)(2,1)S(1)} %get-tuple-element.115), channel_id=1, source_target_pairs={{0,4},{4,8},{8,12},{12,0},{1,5},{5,9},{9,13},{13,1},{2,6},{6,10},{... | collective-permute-start | bytes 393224 | tf_op jit(solution)/shard_map/while/body/eval_jaxpr/ppermute | solution.py:23
  34.9 16.7 %collective-permute-start.1 = (f32[128,1024]{0,1:T(8,128)}, f32[128,1024]{0,1:T(8,128)S(1)}, u32[]{:S(2)}, u32[]{:S(2)}) collective-permute-start(f32[128,1024]{0,1:T(8,128)} %get-tuple-element.116), channel_id=1, source_target_pairs={{0,4},{4,8},{8,12},{12,0},{1,5},{5,9},{9,13},{13,1},{2,6},{6,10},{... | collective-permute-start | bytes 1572872 | tf_op jit(solution)/shard_map/while/body/eval_jaxpr/ppermute | solution.py:23
  52.5 8.2 %collective-permute-start = (bf16[128,512]{1,0:T(8,128)(2,1)S(1)}, bf16[128,512]{1,0:T(8,128)(2,1)S(1)}, u32[]{:S(2)}, u32[]{:S(2)}) collective-permute-start(bf16[128,512]{1,0:T(8,128)(2,1)S(1)} %get-tuple-element.115), channel_id=1, source_target_pairs={{0,4},{4,8},{8,12},{12,0},{1,5},{5,9},{9,13},{13,1},{2,6},{6,10},{... | collective-permute-start | bytes 393224 | tf_op jit(solution)/shard_map/while/body/eval_jaxpr/ppermute | solution.py:23
  52.5 17.7 %collective-permute-start.1 = (f32[128,1024]{0,1:T(8,128)}, f32[128,1024]{0,1:T(8,128)S(1)}, u32[]{:S(2)}, u32[]{:S(2)}) collective-permute-start(f32[128,1024]{0,1:T(8,128)} %get-tuple-element.116), channel_id=1, source_target_pairs={{0,4},{4,8},{8,12},{12,0},{1,5},{5,9},{9,13},{13,1},{2,6},{6,10},{... | collective-permute-start | bytes 1572872 | tf_op jit(solution)/shard_map/while/body/eval_jaxpr/ppermute | solution.py:23
  71.1 8.2 %collective-permute-start = (bf16[128,512]{1,0:T(8,128)(2,1)S(1)}, bf16[128,512]{1,0:T(8,128)(2,1)S(1)}, u32[]{:S(2)}, u32[]{:S(2)}) collective-permute-start(bf16[128,512]{1,0:T(8,128)(2,1)S(1)} %get-tuple-element.115), channel_id=1, source_target_pairs={{0,4},{4,8},{8,12},{12,0},{1,5},{5,9},{9,13},{13,1},{2,6},{6,10},{... | collective-permute-start | bytes 393224 | tf_op jit(solution)/shard_map/while/body/eval_jaxpr/ppermute | solution.py:23
  71.1 16.8 %collective-permute-start.1 = (f32[128,1024]{0,1:T(8,128)}, f32[128,1024]{0,1:T(8,128)S(1)}, u32[]{:S(2)}, u32[]{:S(2)}) collective-permute-start(f32[128,1024]{0,1:T(8,128)} %get-tuple-element.116), channel_id=1, source_target_pairs={{0,4},{4,8},{8,12},{12,0},{1,5},{5,9},{9,13},{13,1},{2,6},{6,10},{... | collective-permute-start | bytes 1572872 | tf_op jit(solution)/shard_map/while/body/eval_jaxpr/ppermute | solution.py:23
  88.8 21.9 %copy-start.6 = (bf16[1024,512]{1,0:T(8,128)(2,1)S(1)}, bf16[1024,512]{1,0:T(8,128)(2,1)}, u32[]{:S(2)}) copy-start(bf16[1024,512]{1,0:T(8,128)(2,1)} %param.25) | copy-start | bytes 3145732
  88.8 68.8 %copy-start.5 = (f32[4,32,512]{2,1,0:T(8,128)S(1)}, f32[4,32,512]{2,1,0:T(8,128)}, u32[]{:S(2)}) copy-start(f32[4,32,512]{2,1,0:T(8,128)} %param.17) | copy-start | bytes 786436
  100.5 10.2 %all-to-all-start = ((f32[4,32,512]{2,1,0:T(8,128)}), f32[4,32,512]{2,1,0:T(8,128)S(1)}, u32[]{:S(2)}, u32[]{:S(2)}) async-start(f32[4,32,512]{2,1,0:T(8,128)} %bitcast.120), calls=%async_computation | async-start | bytes 524288 | tf_op jit(solution)/shard_map/all_to_all | solution.py:77
  103.9 26.9 %all-reduce.3.cloned.1.call-start = ((), (), s32[]{:S(2)}) async-start(), calls=%async_computation.2 | async-start | bytes 524288 | tf_op jit(solution)/shard_map/psum | solution.py:17
  112.4 0.7 copy-start.3
  113.1 44.5 %all-reduce.5.cloned.1.call-start = ((), (), s32[]{:S(2)}) async-start(), calls=%async_computation.3 | async-start | bytes 524288 | tf_op jit(solution)/shard_map/psum | solution.py:17
Sparse Core Ops, SparseCore 0:
  113.2 17.5 all-reduce.2
  133.2 24.3 all-reduce.4
